TPU v7x, 32 devices: a whole 2x2x4 slice. The times are simulated.
32 devices in a mesh: parts: 2 (over y), blk: 4 (over z), sub: 4 (over x, core).
Axes of the slice: x: 2, y: 2, z: 4, core: 2. Of those that a mesh axis runs over, the one named last changes fastest.
Arguments:
- readings: float32 [2, 24576, 256], P(None, ('parts', 'blk', 'sub')), parts along dimension 1, may hold values from -6 to 6
- coverage: int32 [2, 24576, 256], P(None, ('parts', 'blk', 'sub')), parts along dimension 1, may hold values 0 or 1
- pixel_factors: float32 [24576, 256], P(('parts', 'blk', 'sub')), parts along dimension 0, may hold values from -1.5 to 1.5
- date_factors: float32 [2048, 256], P(('parts', 'blk', 'sub')), parts along dimension 0, may hold values from -1.5 to 1.5
Outputs:
- pixel_out: float32 [24576, 256], P(('parts', 'blk', 'sub')), parts along dimension 0
- date_out: float32 [2048, 256], P(('parts', 'blk', 'sub')), parts along dimension 0
There are 2 independent parts, one for each index of `parts`. A program takes and returns all parts, laid end to end along the dimension named above; each array names one. Nothing has to cross between parts.
All inputs are finite; a program needn't handle non-finite values. No bound on the sum of `coverage` on one device may be relied on, other than what follows from the above.
Results may differ from a plain program's by a relative error of at most 0.0001.
Values sent between devices are 32-bit elements; how exact they have to be, the bound alone decides.
No kernel may reach another device: no remote copies, remote signals or barrier semaphores. Data moves between devices by JAX's collectives and lax.ppermute only.
A program may use at most 64 MiB of HBM per device.

v0:
```python
import jax
import jax.numpy as jnp
from jax import lax
from jax.sharding import PartitionSpec as P

STRATA = 2
step_size = 0.05
ridge = 0.1
epsilon = 1e-06


def from_behind(value, axis, steps):
    count = lax.axis_size(axis)
    pairs = [(source, (source + steps) % count) for source in range(count)]
    return lax.ppermute(value, axis, pairs)


def local_terms(values, weights, strip, block):
    hp = lax.Precision.HIGHEST
    predicted = lax.dot_general(strip, block, (((1,), (1,)), ((), ())), precision=hp)
    errors = weights * (values - predicted)
    pixel_grad = -jnp.dot(errors, block, precision=hp) + ridge * strip
    date_part = -lax.dot_general(errors, strip, (((0,), (0,)), ((), ())), precision=hp)
    return (pixel_grad, date_part)


def on_device(readings, coverage, pixel_factors, date_factors):
    strip = pixel_factors
    share_rows = date_factors.shape[0]
    groups = lax.axis_size("sub")
    block_rows = share_rows * groups
    pixel_count = strip.shape[0] * groups * strip.shape[1]
    date_count = block_rows * strip.shape[1]
    share = date_factors
    for stratum in range(STRATA):
        block = lax.all_gather(share, "sub", axis=0, tiled=True)
        values = readings[stratum]
        weights = coverage[stratum].astype(jnp.float32)
        pixel_grad, date_part = local_terms(values, weights, strip, block)
        own_part = lax.psum_scatter(date_part, "sub", scatter_dimension=0, tiled=True)
        date_grad = own_part + ridge * share
        pixel_sq, date_sq = lax.psum(
            (jnp.sum(pixel_grad * pixel_grad), jnp.sum(date_grad * date_grad)), "sub"
        )
        strip = strip - step_size * pixel_grad / jnp.sqrt(pixel_sq / pixel_count + epsilon)
        share = share - step_size * date_grad / jnp.sqrt(date_sq / date_count + epsilon)
        share = from_behind(share, "blk", 1)
    return (strip, share)


def solution(mesh):
    in_specs = (
        P(None, ("parts", "blk", "sub"), None),
        P(None, ("parts", "blk", "sub"), None),
        P(("parts", "blk", "sub"), None),
        P(("parts", "blk", "sub"), None),
    )
    out_specs = (P(("parts", "blk", "sub"), None), P(("parts", "blk", "sub"), None))
    return jax.shard_map(
        on_device, mesh=mesh, in_specs=in_specs, out_specs=out_specs, check_vma=False
    )
```

profile of v0, /device:TPU:0, one launch (start us, length us, event | category | flops | bytes accessed | tf_op | source)
XLA Modules:
  0.0 109.8 jit_solution(7786691914013596123)
XLA Ops:
  7.2 7.4 %all_gather.6 = f32[256,256]{1,0:T(8,128)S(1)} all-gather(f32[64,256]{1,0:T(8,128)} %param.7), channel_id=1, replica_groups=mesh['parts'=2,'blk'=4,'sub'=4] {'sub'}, dimensions={0}, use_global_device_ids=true | all-gather | bytes 327680 | tf_op jit(solution)/shard_map/all_gather | solution.py:36
  14.6 2.5 %fusion.3 = f32[768,256]{1,0:T(8,128)S(1)} fusion(f32[768,256]{1,0:T(8,128)} %param.6, f32[256,256]{1,0:T(8,128)S(1)} %all_gather.6, f32[2,768,256]{2,1,0:T(8,128)} %param.4, s32[2,768,256]{2,1,0:T(8,128)} %param.5), kind=kOutput, calls=%fused_computation.7 | convolution fusion | flops 604569600 | bytes 3407872 | tf_op jit(solution)/shard_map/dot_general | solution.py:20
  17.2 2.1 %convolution_negate_fusion.3 = f32[256,256]{1,0:T(8,128)} fusion(f32[768,256]{1,0:T(8,128)S(1)} %fusion.3, f32[768,256]{1,0:T(8,128)S(1)} %copy-done), kind=kOutput, calls=%fused_computation.9 | convolution fusion | flops 604045312 | bytes 1835008 | tf_op jit(solution)/shard_map/dot_general | solution.py:23
  19.3 0.0 reduce-scatter.5.cloned.1.call-start
  19.4 1.4 %multiply_reduce_fusion.1 = (f32[]{:T(128)}, f32[768,256]{1,0:T(8,128)S(1)}) fusion(f32[768,256]{1,0:T(8,128)S(1)} %copy-done, f32[768,256]{1,0:T(8,128)S(1)} %fusion.3, f32[256,256]{1,0:T(8,128)S(1)} %all_gather.6), kind=kOutput, calls=%fused_computation.13 | convolution fusion | flops 604962816 | bytes 2621444 | tf_op jit(solution)/shard_map/dot_general | solution.py:22
  20.8 20.0 %reduce-scatter.3.cloned.1.call-done = f32[64,256]{1,0:T(8,128)} async-done(((f32[256,256]{1,0:T(8,128)}), f32[64,256]{1,0:T(8,128)}) %reduce-scatter.3.cloned.1.call-update) | async-done | bytes 65552 | tf_op jit(solution)/shard_map/reduce_scatter | solution.py:40
  40.8 1.5 %multiply_reduce_fusion.3 = f32[]{:T(128)} fusion(f32[64,256]{1,0:T(8,128)} %reduce-scatter.3.cloned.1.call-done, f32[64,256]{1,0:T(8,128)S(1)} %copy-done.1), kind=kLoop, calls=%fused_computation.18 | loop fusion | flops 65535 | bytes 131076 | tf_op jit(solution)/shard_map/reduce_sum | solution.py:43
  42.3 6.4 %all-reduce.1 = (f32[]{:T(128)}, f32[]{:T(128)}) all-reduce(f32[]{:T(128)} %get-tuple-element.6, f32[]{:T(128)} %multiply_reduce_fusion.3), channel_id=1, replica_groups=mesh['parts'=2,'blk'=4,'sub'=4] {'sub'}, use_global_device_ids=true, to_apply=%region_1.0 | all-reduce | flops 2 | bytes 16 | tf_op jit(solution)/shard_map/psum | solution.py:42
  50.0 0.9 divide_subtract_fusion.3
  50.9 1.7 %collective-permute-start = (f32[64,256]{1,0:T(8,128)S(1)}, f32[64,256]{1,0:T(8,128)S(1)}, u32[]{:S(2)}, u32[]{:S(2)}) collective-permute-start(f32[64,256]{1,0:T(8,128)S(1)} %divide_subtract_fusion.3), channel_id=1, source_target_pairs={{0,4},{4,8},{8,12},{12,0},{1,5},{5,9},{9,13},{13,1},{2,6},{6,10},{... | collective-permute-start | bytes 196616 | tf_op jit(solution)/shard_map/ppermute | solution.py:15
  52.6 0.1 divide_subtract_fusion.1
  52.7 4.3 %collective-permute-done = f32[64,256]{1,0:T(8,128)S(1)} collective-permute-done((f32[64,256]{1,0:T(8,128)S(1)}, f32[64,256]{1,0:T(8,128)S(1)}, u32[]{:S(2)}, u32[]{:S(2)}) %collective-permute-start) | collective-permute-done | bytes 65568 | tf_op jit(solution)/shard_map/ppermute | solution.py:15
  57.0 5.8 %all_gather.7 = f32[256,256]{1,0:T(8,128)S(1)} all-gather(f32[64,256]{1,0:T(8,128)S(1)} %collective-permute-done), channel_id=1, replica_groups=mesh['parts'=2,'blk'=4,'sub'=4] {'sub'}, dimensions={0}, use_global_device_ids=true | all-gather | bytes 327680 | tf_op jit(solution)/shard_map/all_gather | solution.py:36
  62.8 2.2 %fusion.2 = f32[768,256]{1,0:T(8,128)S(1)} fusion(f32[768,256]{1,0:T(8,128)S(1)} %divide_subtract_fusion.1, f32[256,256]{1,0:T(8,128)S(1)} %all_gather.7, f32[2,768,256]{2,1,0:T(8,128)} %param.4, s32[2,768,256]{2,1,0:T(8,128)} %param.5), kind=kOutput, calls=%fused_computation.5 | convolution fusion | flops 604569600 | bytes 3407872 | tf_op jit(solution)/shard_map/dot_general | solution.py:20
  65.0 2.1 %convolution_negate_fusion.2 = f32[256,256]{1,0:T(8,128)} fusion(f32[768,256]{1,0:T(8,128)S(1)} %fusion.2, f32[768,256]{1,0:T(8,128)S(1)} %divide_subtract_fusion.1), kind=kOutput, calls=%fused_computation.8 | convolution fusion | flops 604045312 | bytes 1835008 | tf_op jit(solution)/shard_map/dot_general | solution.py:23
  67.1 1.4 %multiply_reduce_fusion = (f32[]{:T(128)}, f32[768,256]{1,0:T(8,128)S(1)}) fusion(f32[768,256]{1,0:T(8,128)S(1)} %divide_subtract_fusion.1, f32[768,256]{1,0:T(8,128)S(1)} %fusion.2, f32[256,256]{1,0:T(8,128)S(1)} %all_gather.7), kind=kOutput, calls=%fused_computation.11 | convolution fusion | flops 604962816 | bytes 2621444 | tf_op jit(solution)/shard_map/dot_general | solution.py:22
  68.5 17.6 %reduce-scatter.5.cloned.1.call-done = f32[64,256]{1,0:T(8,128)} async-done(((f32[256,256]{1,0:T(8,128)}), f32[64,256]{1,0:T(8,128)}) %reduce-scatter.5.cloned.1.call-update) | async-done | bytes 65552 | tf_op jit(solution)/shard_map/reduce_scatter | solution.py:40
  86.1 1.5 %multiply_reduce_fusion.2 = f32[]{:T(128)} fusion(f32[64,256]{1,0:T(8,128)} %reduce-scatter.5.cloned.1.call-done, f32[64,256]{1,0:T(8,128)S(1)} %collective-permute-done), kind=kLoop, calls=%fused_computation.15 | loop fusion | flops 65535 | bytes 131076 | tf_op jit(solution)/shard_map/reduce_sum | solution.py:43
  87.6 6.4 %all-reduce = (f32[]{:T(128)}, f32[]{:T(128)}) all-reduce(f32[]{:T(128)} %get-tuple-element.8, f32[]{:T(128)} %multiply_reduce_fusion.2), channel_id=1, replica_groups=mesh['parts'=2,'blk'=4,'sub'=4] {'sub'}, use_global_device_ids=true, to_apply=%region_6.0 | all-reduce | flops 2 | bytes 16 | tf_op jit(solution)/shard_map/psum | solution.py:42
  95.3 0.9 divide_subtract_fusion.2
  96.2 1.7 %collective-permute-start.1 = (f32[64,256]{1,0:T(8,128)S(1)}, f32[64,256]{1,0:T(8,128)S(1)}, u32[]{:S(2)}, u32[]{:S(2)}) collective-permute-start(f32[64,256]{1,0:T(8,128)S(1)} %divide_subtract_fusion.2), channel_id=1, source_target_pairs={{0,4},{4,8},{8,12},{12,0},{1,5},{5,9},{9,13},{13,1},{2,6},{6,10},{... | collective-permute-start | bytes 196616 | tf_op jit(solution)/shard_map/ppermute | solution.py:15
  97.9 1.0 divide_subtract_fusion
  98.9 3.4 %collective-permute-done.1 = f32[64,256]{1,0:T(8,128)S(1)} collective-permute-done((f32[64,256]{1,0:T(8,128)S(1)}, f32[64,256]{1,0:T(8,128)S(1)}, u32[]{:S(2)}, u32[]{:S(2)}) %collective-permute-start.1) | collective-permute-done | bytes 65568 | tf_op jit(solution)/shard_map/ppermute | solution.py:15
  102.3 0.6 copy.7
  (7 shorter events, 0.1 us)
Async XLA Ops:
  7.2 33.6 %reduce-scatter.3.cloned.1.call-start = ((), (), s32[]{:S(2)}) async-start(), calls=%async_computation.2 | async-start | bytes 327680 | tf_op jit(solution)/shard_map/reduce_scatter | solution.py:40
  14.6 2.5 %copy-start = (f32[768,256]{1,0:T(8,128)S(1)}, f32[768,256]{1,0:T(8,128)}, u32[]{:S(2)}) copy-start(f32[768,256]{1,0:T(8,128)} %param.6) | copy-start | bytes 2359300
  19.3 21.5 %copy-start.1 = (f32[64,256]{1,0:T(8,128)S(1)}, f32[64,256]{1,0:T(8,128)}, u32[]{:S(2)}) copy-start(f32[64,256]{1,0:T(8,128)} %param.7) | copy-start | bytes 196612
  19.3 66.8 %reduce-scatter.5.cloned.1.call-start = ((), (), s32[]{:S(2)}) async-start(), calls=%async_computation.3 | async-start | bytes 327680 | tf_op jit(solution)/shard_map/reduce_scatter | solution.py:40
  50.9 6.1 %collective-permute-start = (f32[64,256]{1,0:T(8,128)S(1)}, f32[64,256]{1,0:T(8,128)S(1)}, u32[]{:S(2)}, u32[]{:S(2)}) collective-permute-start(f32[64,256]{1,0:T(8,128)S(1)} %divide_subtract_fusion.3), channel_id=1, source_target_pairs={{0,4},{4,8},{8,12},{12,0},{1,5},{5,9},{9,13},{13,1},{2,6},{6,10},{... | collective-permute-start | bytes 196616 | tf_op jit(solution)/shard_map/ppermute | solution.py:15
  96.2 6.1 %collective-permute-start.1 = (f32[64,256]{1,0:T(8,128)S(1)}, f32[64,256]{1,0:T(8,128)S(1)}, u32[]{:S(2)}, u32[]{:S(2)}) collective-permute-start(f32[64,256]{1,0:T(8,128)S(1)} %divide_subtract_fusion.2), channel_id=1, source_target_pairs={{0,4},{4,8},{8,12},{12,0},{1,5},{5,9},{9,13},{13,1},{2,6},{6,10},{... | collective-permute-start | bytes 196616 | tf_op jit(solution)/shard_map/ppermute | solution.py:15
Sparse Core Ops, SparseCore 0:
  19.4 21.3 reduce-scatter.2
  67.2 18.8 reduce-scatter.4
where the time goes:
time: 110 us
  waiting for transfers between devices  45.3 us (41%)
  blocking collectives  25.9 us (24%)
  between operations  16.8 us (15%)
  matrix products  11.7 us (11%)
  other arithmetic  5.73 us (5%)
  starting transfers between devices  3.54 us (3%)
    reduce_scatter x2, waiting for transfers between devices, on_device(): lax.psum_scatter(date_part, 'sub', scatter_dimension=0, tiled=True)  37.6 us
    all_gather x2, blocking collectives, on_device(): block = lax.all_gather(share, 'sub', axis=0, tiled=True)  13.2 us
    psum x2, blocking collectives, on_device(): lax.psum((jnp.sum(pixel_grad * pixel_grad), jnp.sum(date_grad * date_grad...  12.7 us
    ppermute x2, waiting for transfers between devices, from_behind(): return lax.ppermute(value, axis, pairs)  7.68 us
    dot_general x2, matrix products, local_terms(): lax.dot_general(strip, block, (((1,), (1,)), ((), ())), precision=hp)  4.68 us
    dot_general x2, matrix products, local_terms(): lax.dot_general(errors, strip, (((0,), (0,)), ((), ())), precision=hp)  4.24 us
    ppermute x2, starting transfers between devices, from_behind(): return lax.ppermute(value, axis, pairs)  3.46 us
    reduce_sum x2, other arithmetic, on_device(): jnp.sum(date_grad * date_grad)  2.92 us
  transfers between devices with their start and end apart: 4, of which 4 were waited for; matrix products, arithmetic and copies ran while one was open for 4% of the time, Pallas kernels for 0%

commit v1 on v0

--- a/solution.py
+++ b/solution.py
@@ -7,6 +7,17 @@
 step_size = 0.05
 ridge = 0.1
 epsilon = 1e-06
+
+
+def gather_by_hops(x, axis, dim):
+    size = lax.axis_size(axis)
+    right = [(i, (i + 1) % size) for i in range(size)]
+    shards = [x]
+    for stride in range(1, size):
+        shards = [lax.ppermute(shards[0], axis, right), *shards]
+    whole = jnp.concatenate(shards, axis=dim)
+    shift = (lax.axis_index(axis) + 1) * shards[-1].shape[dim]
+    return jnp.roll(whole, shift, axis=dim)
 
 
 def from_behind(value, axis, steps):
@@ -33,7 +44,7 @@
     date_count = block_rows * strip.shape[1]
     share = date_factors
     for stratum in range(STRATA):
-        block = lax.all_gather(share, "sub", axis=0, tiled=True)
+        block = gather_by_hops(share, "sub", 0)
         values = readings[stratum]
         weights = coverage[stratum].astype(jnp.float32)
         pixel_grad, date_part = local_terms(values, weights, strip, block)

time: 110 us -> 120 us (1.091)
  waiting for transfers between devices: 45.3 us -> 65.8 us
  blocking collectives: 25.9 us -> 12.7 us
  other arithmetic: 5.73 us -> 7.34 us
  matrix products: 11.7 us -> 10.1 us
  local copies, waits for them, and re-layouts: 0.64 us -> 2.03 us
    ppermute x0 -> x6, waiting for transfers between devices: none -> 20.2 us  [gather_by_hops(): shards = [lax.ppermute(shards[0], axis, right), *shards]]
    all_gather x2 -> x0, blocking collectives: 13.2 us -> none  [on_device(): block = lax.all_gather(share, 'sub', axis=0, tiled=True)]
    dot_general x2, matrix products: 4.68 us -> 3.04 us  [local_terms(): lax.dot_general(strip, block, (((1,), (1,)), ((), ())), precision=hp)]
    concatenate x0 -> x2, other arithmetic: none -> 1.62 us  [gather_by_hops(): return jnp.roll(whole, shift, axis=dim)]
  transfers between devices with their start and end apart: 4 -> 10, of which waited for: 4 -> 10; matrix products, arithmetic and copies ran while one was open for 4% -> 4% of each run, Pallas kernels for 0% -> 0%
where the time goes in v1:
time: 120 us; the launch traced here: 119 us
  waiting for transfers between devices  65.8 us (55%)
  between operations  16.9 us (14%)
  blocking collectives  12.7 us (11%)
  matrix products  10.1 us (8%)
  other arithmetic  7.34 us (6%)
  starting transfers between devices  4.33 us (4%)
  local copies, waits for them, and re-layouts  2.03 us (2%)
    reduce_scatter x2, waiting for transfers between devices, on_device(): lax.psum_scatter(date_part, 'sub', scatter_dimension=0, tiled=True)  37.8 us
    ppermute x6, waiting for transfers between devices, gather_by_hops(): shards = [lax.ppermute(shards[0], axis, right), *shards]  20.2 us
    psum x2, blocking collectives, on_device(): lax.psum((jnp.sum(pixel_grad * pixel_grad), jnp.sum(date_grad * date_grad...  12.7 us
    ppermute x2, waiting for transfers between devices, from_behind(): return lax.ppermute(value, axis, pairs)  7.76 us
    dot_general x2, matrix products, local_terms(): lax.dot_general(errors, strip, (((0,), (0,)), ((), ())), precision=hp)  3.63 us
    ppermute x2, starting transfers between devices, from_behind(): return lax.ppermute(value, axis, pairs)  3.48 us
    dot_general x2, matrix products, local_terms(): pixel_grad = -jnp.dot(errors, block, precision=hp) + ridge * strip  3.44 us
    dot_general x2, matrix products, local_terms(): lax.dot_general(strip, block, (((1,), (1,)), ((), ())), precision=hp)  3.04 us
  transfers between devices with their start and end apart: 10, of which 10 were waited for; matrix products, arithmetic and copies ran while one was open for 4% of the time, Pallas kernels for 0%

profile of v1, /device:TPU:0, one launch (start us, length us, event | category | flops | bytes accessed | tf_op | source)
XLA Modules:
  0.0 119.2 jit_solution(16735285917343817295)
XLA Ops:
  7.8 4.1 %collective-permute-done = f32[64,256]{1,0:T(8,128)S(1)} collective-permute-done((f32[64,256]{1,0:T(8,128)}, f32[64,256]{1,0:T(8,128)S(1)}, u32[]{:S(2)}, u32[]{:S(2)}) %collective-permute-start) | collective-permute-done | bytes 65568 | tf_op jit(solution)/shard_map/ppermute | solution.py:17
  12.0 3.5 %collective-permute-done.1 = f32[64,256]{1,0:T(8,128)S(1)} collective-permute-done((f32[64,256]{1,0:T(8,128)S(1)}, f32[64,256]{1,0:T(8,128)S(1)}, u32[]{:S(2)}, u32[]{:S(2)}) %collective-permute-start.1) | collective-permute-done | bytes 65568 | tf_op jit(solution)/shard_map/ppermute | solution.py:17
  17.0 2.3 %collective-permute-done.2 = f32[64,256]{1,0:T(8,128)} collective-permute-done((f32[64,256]{1,0:T(8,128)S(1)}, f32[64,256]{1,0:T(8,128)}, u32[]{:S(2)}, u32[]{:S(2)}) %collective-permute-start.2) | collective-permute-done | bytes 65568 | tf_op jit(solution)/shard_map/ppermute | solution.py:17
  19.3 1.2 %fusion.15 = f32[256,256]{1,0:T(8,128)S(1)} fusion(s32[]{:T(128)S(6)} %select_n.13, f32[64,256]{1,0:T(8,128)} %collective-permute-done.2, f32[64,256]{1,0:T(8,128)} %copy-done.2, f32[64,256]{1,0:T(8,128)S(1)} %collective-permute-done, f32[64,256]{1,0:T(8,128)S(1)} %copy-done.1), kind=kLoop, calls=%fused_computation.41 | loop fusion | flops 458752 | bytes 524292 | tf_op jit(solution)/shard_map/jit(_roll_dynamic)/concatenate | solution.py:20
  21.4 1.5 %convolution_negate_fusion.3 = f32[256,256]{1,0:T(8,128)} fusion(f32[768,256]{0,1:T(8,128)S(1)} %fusion.1, f32[768,256]{1,0:T(8,128)S(1)} %copy-done), kind=kOutput, calls=%fused_computation.10 | convolution fusion | flops 604045312 | bytes 1835008 | tf_op jit(solution)/shard_map/dot_general | solution.py:34
  23.0 2.0 %multiply_reduce_fusion.1 = (f32[]{:T(128)}, f32[768,256]{1,0:T(8,128)S(1)}) fusion(f32[768,256]{1,0:T(8,128)S(1)} %copy-done, f32[768,256]{0,1:T(8,128)S(1)} %fusion.1, f32[256,256]{1,0:T(8,128)S(1)} %fusion.15), kind=kOutput, calls=%fused_computation.14 | convolution fusion | flops 604962816 | bytes 2621444 | tf_op jit(solution)/shard_map/dot_general | solution.py:33
  25.0 20.2 %reduce-scatter.3.cloned.1.call-done = f32[64,256]{1,0:T(8,128)} async-done(((f32[256,256]{1,0:T(8,128)}), f32[64,256]{1,0:T(8,128)}) %reduce-scatter.3.cloned.1.call-update) | async-done | bytes 65552 | tf_op jit(solution)/shard_map/reduce_scatter | solution.py:51
  45.2 1.5 %multiply_reduce_fusion.3 = f32[]{:T(128)} fusion(f32[64,256]{1,0:T(8,128)} %reduce-scatter.3.cloned.1.call-done, f32[64,256]{1,0:T(8,128)S(1)} %copy-done.1), kind=kLoop, calls=%fused_computation.49 | loop fusion | flops 65535 | bytes 131076 | tf_op jit(solution)/shard_map/reduce_sum | solution.py:54
  46.7 6.4 %all-reduce.1 = (f32[]{:T(128)}, f32[]{:T(128)}) all-reduce(f32[]{:T(128)} %get-tuple-element.7, f32[]{:T(128)} %multiply_reduce_fusion.3), channel_id=1, replica_groups=mesh['parts'=2,'blk'=4,'sub'=4] {'sub'}, use_global_device_ids=true, to_apply=%region_1.3 | all-reduce | flops 2 | bytes 16 | tf_op jit(solution)/shard_map/psum | solution.py:53
  54.6 1.8 %collective-permute-start.3 = (f32[64,256]{1,0:T(8,128)S(1)}, f32[64,256]{1,0:T(8,128)S(1)}, u32[]{:S(2)}, u32[]{:S(2)}) collective-permute-start(f32[64,256]{1,0:T(8,128)S(1)} %divide_subtract_fusion.3), channel_id=1, source_target_pairs={{0,4},{4,8},{8,12},{12,0},{1,5},{5,9},{9,13},{13,1},{2,6},{6,10},{... | collective-permute-start | bytes 196616 | tf_op jit(solution)/shard_map/ppermute | solution.py:26
  56.3 4.4 %collective-permute-done.3 = f32[64,256]{1,0:T(8,128)S(1)} collective-permute-done((f32[64,256]{1,0:T(8,128)S(1)}, f32[64,256]{1,0:T(8,128)S(1)}, u32[]{:S(2)}, u32[]{:S(2)}) %collective-permute-start.3) | collective-permute-done | bytes 65568 | tf_op jit(solution)/shard_map/ppermute | solution.py:26
  60.7 3.7 %collective-permute-done.4 = f32[64,256]{1,0:T(8,128)S(1)} collective-permute-done((f32[64,256]{1,0:T(8,128)S(1)}, f32[64,256]{1,0:T(8,128)S(1)}, u32[]{:S(2)}, u32[]{:S(2)}) %collective-permute-start.4) | collective-permute-done | bytes 65568 | tf_op jit(solution)/shard_map/ppermute | solution.py:17
  65.1 3.0 %collective-permute-done.5 = f32[64,256]{1,0:T(8,128)S(1)} collective-permute-done((f32[64,256]{1,0:T(8,128)S(1)}, f32[64,256]{1,0:T(8,128)S(1)}, u32[]{:S(2)}, u32[]{:S(2)}) %collective-permute-start.5) | collective-permute-done | bytes 65568 | tf_op jit(solution)/shard_map/ppermute | solution.py:17
  68.2 3.6 %collective-permute-done.6 = f32[64,256]{1,0:T(8,128)S(1)} collective-permute-done((f32[64,256]{1,0:T(8,128)S(1)}, f32[64,256]{1,0:T(8,128)S(1)}, u32[]{:S(2)}, u32[]{:S(2)}) %collective-permute-start.6) | collective-permute-done | bytes 65568 | tf_op jit(solution)/shard_map/ppermute | solution.py:17
  72.2 2.2 %fusion.4 = f32[768,256]{1,0:T(8,128)S(1)} fusion(f32[768,256]{1,0:T(8,128)S(1)} %divide_subtract_fusion.1, f32[256,256]{1,0:T(8,128)S(1)} %fusion.8, f32[2,768,256]{2,1,0:T(8,128)} %param.6, s32[2,768,256]{2,1,0:T(8,128)} %param.7), kind=kOutput, calls=%fused_computation.8 | convolution fusion | flops 604569600 | bytes 3407872 | tf_op jit(solution)/shard_map/dot_general | solution.py:31
  74.4 2.1 %convolution_negate_fusion.2 = f32[256,256]{1,0:T(8,128)} fusion(f32[768,256]{1,0:T(8,128)S(1)} %fusion.4, f32[768,256]{1,0:T(8,128)S(1)} %divide_subtract_fusion.1), kind=kOutput, calls=%fused_computation.9 | convolution fusion | flops 604045312 | bytes 1835008 | tf_op jit(solution)/shard_map/dot_general | solution.py:34
  76.5 1.4 %multiply_reduce_fusion = (f32[]{:T(128)}, f32[768,256]{1,0:T(8,128)S(1)}) fusion(f32[768,256]{1,0:T(8,128)S(1)} %divide_subtract_fusion.1, f32[768,256]{1,0:T(8,128)S(1)} %fusion.4, f32[256,256]{1,0:T(8,128)S(1)} %fusion.8), kind=kOutput, calls=%fused_computation.12 | convolution fusion | flops 604962816 | bytes 2621444 | tf_op jit(solution)/shard_map/dot_general | solution.py:33
  78.0 17.6 %reduce-scatter.5.cloned.1.call-done = f32[64,256]{1,0:T(8,128)} async-done(((f32[256,256]{1,0:T(8,128)}), f32[64,256]{1,0:T(8,128)}) %reduce-scatter.5.cloned.1.call-update) | async-done | bytes 65552 | tf_op jit(solution)/shard_map/reduce_scatter | solution.py:51
  95.5 1.5 %multiply_reduce_fusion.2 = f32[]{:T(128)} fusion(f32[64,256]{1,0:T(8,128)} %reduce-scatter.5.cloned.1.call-done, f32[64,256]{1,0:T(8,128)S(1)} %collective-permute-done.3), kind=kLoop, calls=%fused_computation.46 | loop fusion | flops 65535 | bytes 131076 | tf_op jit(solution)/shard_map/reduce_sum | solution.py:54
  97.0 6.4 %all-reduce = (f32[]{:T(128)}, f32[]{:T(128)}) all-reduce(f32[]{:T(128)} %get-tuple-element.9, f32[]{:T(128)} %multiply_reduce_fusion.2), channel_id=1, replica_groups=mesh['parts'=2,'blk'=4,'sub'=4] {'sub'}, use_global_device_ids=true, to_apply=%region_6.8 | all-reduce | flops 2 | bytes 16 | tf_op jit(solution)/shard_map/psum | solution.py:53
  104.8 0.9 divide_subtract_fusion.2
  105.6 1.7 %collective-permute-start.7 = (f32[64,256]{1,0:T(8,128)S(1)}, f32[64,256]{1,0:T(8,128)S(1)}, u32[]{:S(2)}, u32[]{:S(2)}) collective-permute-start(f32[64,256]{1,0:T(8,128)S(1)} %divide_subtract_fusion.2), channel_id=1, source_target_pairs={{0,4},{4,8},{8,12},{12,0},{1,5},{5,9},{9,13},{13,1},{2,6},{6,10},{... | collective-permute-start | bytes 196616 | tf_op jit(solution)/shard_map/ppermute | solution.py:26
  107.3 1.0 divide_subtract_fusion
  108.3 3.4 %collective-permute-done.7 = f32[64,256]{1,0:T(8,128)S(1)} collective-permute-done((f32[64,256]{1,0:T(8,128)S(1)}, f32[64,256]{1,0:T(8,128)S(1)}, u32[]{:S(2)}, u32[]{:S(2)}) %collective-permute-start.7) | collective-permute-done | bytes 65568 | tf_op jit(solution)/shard_map/ppermute | solution.py:26
  (27 shorter events, 5.1 us)
Async XLA Ops:
  7.2 8.4 %slice-start = ((f32[2,768,256]{2,1,0:T(8,128)}), f32[1,768,256]{2,1,0:T(8,128)S(1)}, s32[]{:S(2)}) async-start(f32[2,768,256]{2,1,0:T(8,128)} %param.6), calls=%async_computation.4 | async-start | bytes 1572864 | tf_op jit(solution)/shard_map/slice | solution.py:48
  7.2 38.0 %reduce-scatter.3.cloned.1.call-start = ((), (), s32[]{:S(2)}) async-start(), calls=%async_computation.2 | async-start | bytes 327680 | tf_op jit(solution)/shard_map/reduce_scatter | solution.py:51
  7.2 4.6 %collective-permute-start = (f32[64,256]{1,0:T(8,128)}, f32[64,256]{1,0:T(8,128)S(1)}, u32[]{:S(2)}, u32[]{:S(2)}) collective-permute-start(f32[64,256]{1,0:T(8,128)} %param.9), channel_id=1, source_target_pairs={{0,1},{1,2},{2,3},{3,0},{4,5},{5,6},{6,7},{7,4},{8,9},{9,10},{10,1... | collective-permute-start | bytes 196616 | tf_op jit(solution)/shard_map/ppermute | solution.py:17
  11.8 3.7 %collective-permute-start.1 = (f32[64,256]{1,0:T(8,128)S(1)}, f32[64,256]{1,0:T(8,128)S(1)}, u32[]{:S(2)}, u32[]{:S(2)}) collective-permute-start(f32[64,256]{1,0:T(8,128)S(1)} %collective-permute-done), channel_id=1, source_target_pairs={{0,1},{1,2},{2,3},{3,0},{4,5},{5,6},{6,7},{7,4},{8,9},{9,10},{10,1... | collective-permute-start | bytes 196616 | tf_op jit(solution)/shard_map/ppermute | solution.py:17
  15.5 0.6 copy-start.2
  15.5 3.8 %collective-permute-start.2 = (f32[64,256]{1,0:T(8,128)S(1)}, f32[64,256]{1,0:T(8,128)}, u32[]{:S(2)}, u32[]{:S(2)}) collective-permute-start(f32[64,256]{1,0:T(8,128)S(1)} %collective-permute-done.1), channel_id=1, source_target_pairs={{0,1},{1,2},{2,3},{3,0},{4,5},{5,6},{6,7},{7,4},{8,9},{9,10},{10,1... | collective-permute-start | bytes 196616 | tf_op jit(solution)/shard_map/ppermute | solution.py:17
  15.6 1.1 slice-start.1
  16.2 3.2 %copy-start.1 = (f32[64,256]{1,0:T(8,128)S(1)}, f32[64,256]{1,0:T(8,128)}, u32[]{:S(2)}) copy-start(f32[64,256]{1,0:T(8,128)} %param.9) | copy-start | bytes 196612
  16.2 4.4 %copy-start = (f32[768,256]{1,0:T(8,128)S(1)}, f32[768,256]{1,0:T(8,128)}, u32[]{:S(2)}) copy-start(f32[768,256]{1,0:T(8,128)} %param.8) | copy-start | bytes 2359300
  22.9 72.6 %reduce-scatter.5.cloned.1.call-start = ((), (), s32[]{:S(2)}) async-start(), calls=%async_computation.3 | async-start | bytes 327680 | tf_op jit(solution)/shard_map/reduce_scatter | solution.py:51
  54.6 6.1 %collective-permute-start.3 = (f32[64,256]{1,0:T(8,128)S(1)}, f32[64,256]{1,0:T(8,128)S(1)}, u32[]{:S(2)}, u32[]{:S(2)}) collective-permute-start(f32[64,256]{1,0:T(8,128)S(1)} %divide_subtract_fusion.3), channel_id=1, source_target_pairs={{0,4},{4,8},{8,12},{12,0},{1,5},{5,9},{9,13},{13,1},{2,6},{6,10},{... | collective-permute-start | bytes 196616 | tf_op jit(solution)/shard_map/ppermute | solution.py:26
  60.7 3.7 %collective-permute-start.4 = (f32[64,256]{1,0:T(8,128)S(1)}, f32[64,256]{1,0:T(8,128)S(1)}, u32[]{:S(2)}, u32[]{:S(2)}) collective-permute-start(f32[64,256]{1,0:T(8,128)S(1)} %collective-permute-done.3), channel_id=1, source_target_pairs={{0,1},{1,2},{2,3},{3,0},{4,5},{5,6},{6,7},{7,4},{8,9},{9,10},{10,1... | collective-permute-start | bytes 196616 | tf_op jit(solution)/shard_map/ppermute | solution.py:17
  64.4 3.7 %collective-permute-start.5 = (f32[64,256]{1,0:T(8,128)S(1)}, f32[64,256]{1,0:T(8,128)S(1)}, u32[]{:S(2)}, u32[]{:S(2)}) collective-permute-start(f32[64,256]{1,0:T(8,128)S(1)} %collective-permute-done.4), channel_id=1, source_target_pairs={{0,1},{1,2},{2,3},{3,0},{4,5},{5,6},{6,7},{7,4},{8,9},{9,10},{10,1... | collective-permute-start | bytes 196616 | tf_op jit(solution)/shard_map/ppermute | solution.py:17
  68.1 3.7 %collective-permute-start.6 = (f32[64,256]{1,0:T(8,128)S(1)}, f32[64,256]{1,0:T(8,128)S(1)}, u32[]{:S(2)}, u32[]{:S(2)}) collective-permute-start(f32[64,256]{1,0:T(8,128)S(1)} %collective-permute-done.5), channel_id=1, source_target_pairs={{0,1},{1,2},{2,3},{3,0},{4,5},{5,6},{6,7},{7,4},{8,9},{9,10},{10,1... | collective-permute-start | bytes 196616 | tf_op jit(solution)/shard_map/ppermute | solution.py:17
  105.6 6.1 %collective-permute-start.7 = (f32[64,256]{1,0:T(8,128)S(1)}, f32[64,256]{1,0:T(8,128)S(1)}, u32[]{:S(2)}, u32[]{:S(2)}) collective-permute-start(f32[64,256]{1,0:T(8,128)S(1)} %divide_subtract_fusion.2), channel_id=1, source_target_pairs={{0,4},{4,8},{8,12},{12,0},{1,5},{5,9},{9,13},{13,1},{2,6},{6,10},{... | collective-permute-start | bytes 196616 | tf_op jit(solution)/shard_map/ppermute | solution.py:26
Sparse Core Ops, SparseCore 0:
  23.1 22.0 reduce-scatter.2
  76.7 18.8 reduce-scatter.4
